TPU v7x, 256 devices: a whole 4x4x8 slice. The times are simulated.
256 devices in a mesh: narrow: 8 (over x, z_lo), wide: 32 (over y, z_hi, core).
Axes of the slice: x: 4, y: 4, z: 8 (z_hi: 4, z_lo: 2; z = z_hi * 2 + z_lo), core: 2. Of those that a mesh axis runs over, the one named last changes fastest.
Arguments:
- basis: bfloat16 [128, 32, 512, 128], P(None, 'narrow', 'wide'), may hold values from -6 to 6
- rhs: bfloat16 [32, 512, 128], P('narrow', 'wide'), may hold values from -48 to 48
- coeffs: float32 [4, 32, 512, 128], P(None, 'narrow', 'wide'), may hold values from 0.25 to 4
- rows: int32 [4, 32, 512, 128], P(None, 'narrow', 'wide'), may hold values from 0 to 255
- signs: int32 [4, 32, 512, 128], P(None, 'narrow', 'wide'), may hold values from 0 to 1
- params: float32 [256, 4], P(('narrow', 'wide')), may hold values from 0.25 to 4
- order: int32 [256], replicated, may hold values from 0 to 255, each once
Outputs:
- fields: bfloat16 [256, 32, 512, 128], P(None, 'narrow', 'wide')
Inputs may be any that keep to these rules, and one draw needn't show every extreme that they name: `order`: each point number appears exactly once.
All inputs are finite; a program needn't handle non-finite values.
Results may differ from a plain program's by a relative error of at most 0.0056.
Values may be sent and summed in bfloat16 or wider, within the bound.
No kernel may reach another device: no remote copies, remote signals or barrier semaphores. Data moves between devices by JAX's collectives and lax.ppermute only.
A program may use at most 64 MiB of HBM per device.

v0:
```python
import jax
import jax.numpy as jnp
from jax import lax
from jax.sharding import PartitionSpec as P

K = 128
M = 1024
TERMS = 4
NNZ = 4


def extended(cells, sides, width):
    for axis, dim in sides:
        count = lax.axis_size(axis)
        ends = count - 1
        head = lax.slice_in_dim(cells, 0, width, axis=dim)
        tail = lax.slice_in_dim(cells, cells.shape[dim] - width, cells.shape[dim], axis=dim)
        cells = jnp.concatenate(
            [
                lax.ppermute(tail, axis, [(i, (i + 1) % count) for i in range(ends)]),
                cells,
                lax.ppermute(head, axis, [((i + 1) % count, i) for i in range(ends)]),
            ],
            axis=dim,
        )
    return cells


def column_products(sketched, sketched_rhs):
    dims = (((0,), (0,)), ((), ()))
    gram_matrix = lax.dot_general(
        sketched,
        sketched,
        dims,
        precision=lax.Precision.HIGHEST,
        preferred_element_type=jnp.float32,
    )
    projected = lax.dot_general(
        sketched,
        sketched_rhs,
        dims,
        precision=lax.Precision.HIGHEST,
        preferred_element_type=jnp.float32,
    )
    return (gram_matrix, projected)


def solve_points(point_params, gram_matrix, projected):
    gram_blocks = gram_matrix.reshape(TERMS, K, TERMS, K)
    proj_blocks = projected.reshape(TERMS, K)
    pair_weight = point_params[:, :, None] * point_params[:, None, :]
    normal = jnp.einsum("pqr,qirj->pij", pair_weight, gram_blocks, precision=lax.Precision.HIGHEST)
    right_side = jnp.einsum("pq,qi->pi", point_params, proj_blocks, precision=lax.Precision.HIGHEST)
    lower_factor = jnp.linalg.cholesky(normal)
    forward = lax.linalg.triangular_solve(
        lower_factor, right_side[:, :, None], left_side=True, lower=True
    )
    solved = lax.linalg.triangular_solve(
        lower_factor, forward, left_side=True, lower=True, transpose_a=True
    )
    return solved[:, :, 0]


def per_device(basis, rhs, coeffs, rows, signs, params, order):
    cell_count = basis.shape[1] * basis.shape[2] * basis.shape[3]
    padded = extended(basis, (("narrow", 1), ("wide", 2)), 1).astype(jnp.float32)
    centre = padded[:, 1:-1, 1:-1, :]
    along_x = 2.0 * centre - padded[:, :-2, 1:-1, :] - padded[:, 2:, 1:-1, :]
    along_y = 2.0 * centre - padded[:, 1:-1, :-2, :] - padded[:, 1:-1, 2:, :]
    z_padded = jnp.pad(centre, ((0, 0), (0, 0), (0, 0), (1, 1)))
    along_z = 2.0 * centre - z_padded[..., :-2] - z_padded[..., 2:]
    terms = jnp.stack(
        [coeffs[0] * centre, coeffs[1] * along_x, coeffs[2] * along_y, coeffs[3] * along_z]
    )
    terms = terms.astype(jnp.bfloat16).reshape(TERMS * K, cell_count)
    row_block = M // NNZ
    flat_rows = rows.reshape(NNZ, cell_count)
    sign_values = ((2 * signs - 1).astype(jnp.float32) * 0.5).reshape(NNZ, cell_count)
    flat_rhs = rhs.reshape(cell_count)
    block_cells = max(min(1024, cell_count), cell_count // 16)
    block_count = cell_count // block_cells
    row_slots = lax.broadcasted_iota(jnp.int32, (1, row_block, 1), 1)

    def accumulate(turn_index, carry):
        sketch_sum, rhs_sum = carry
        offset = turn_index * block_cells
        hashed_rows = lax.dynamic_slice_in_dim(flat_rows, offset, block_cells, 1)
        hashed_signs = lax.dynamic_slice_in_dim(sign_values, offset, block_cells, 1)
        hashed = jnp.where(row_slots == hashed_rows[:, None, :], hashed_signs[:, None, :], 0.0)
        hashed = hashed.astype(jnp.bfloat16).reshape(M, block_cells)
        columns = lax.dynamic_slice_in_dim(terms, offset, block_cells, 1)
        sketch_sum = sketch_sum + lax.dot_general(
            hashed, columns, (((1,), (1,)), ((), ())), preferred_element_type=jnp.float32
        )
        source = lax.dynamic_slice_in_dim(flat_rhs, offset, block_cells, 0)
        rhs_sum = rhs_sum + jnp.dot(hashed, source, preferred_element_type=jnp.float32)
        return (sketch_sum, rhs_sum)

    start = (jnp.zeros((M, TERMS * K), jnp.float32), jnp.zeros((M,), jnp.float32))
    sketched, sketched_rhs = lax.fori_loop(0, block_count, accumulate, start)
    sketched, sketched_rhs = lax.psum((sketched, sketched_rhs), ("narrow", "wide"))
    gram_matrix, projected = column_products(sketched, sketched_rhs)
    own_coef = solve_points(params, gram_matrix, projected).astype(jnp.bfloat16)
    all_coef = lax.all_gather(own_coef, ("narrow", "wide"), axis=0, tiled=True)
    point_total = all_coef.shape[0]
    picker = (order[:, None] == lax.broadcasted_iota(jnp.int32, (1, point_total), 1)).astype(
        jnp.bfloat16
    )
    picked = jnp.dot(picker, all_coef, preferred_element_type=jnp.float32).astype(jnp.bfloat16)
    fields = jnp.dot(picked, basis.reshape(K, cell_count), preferred_element_type=jnp.float32)
    return fields.astype(jnp.bfloat16).reshape(
        point_total, basis.shape[1], basis.shape[2], basis.shape[3]
    )


def solution(mesh):
    in_specs = (
        P(None, "narrow", "wide", None),
        P("narrow", "wide", None),
        P(None, "narrow", "wide", None),
        P(None, "narrow", "wide", None),
        P(None, "narrow", "wide", None),
        P(("narrow", "wide"), None),
        P(),
    )
    out_specs = P(None, "narrow", "wide", None)
    return jax.shard_map(
        per_device, mesh=mesh, in_specs=in_specs, out_specs=out_specs, check_vma=False
    )
```

profile of v0, /device:TPU:1, one launch (start us, length us, event | category | flops | bytes accessed | tf_op | source)
XLA Modules:
  0.0 799.9 jit_solution(9524437281529108941)
XLA Ops:
  6.5 1.6 fusion.34
  8.1 0.9 copy.40
  9.0 5.1 collective-permute-start
  14.3 1.3 collective-permute-start.1
  15.8 8.4 %collective-permute-done = bf16[128,1,16,128]{3,0,2,1:T(8,128)(2,1)} collective-permute-done((bf16[128,1,16,128]{3,0,2,1:T(8,128)(2,1)}, bf16[128,1,16,128]{3,0,2,1:T(8,128)(2,1)}, u32[]{:S(2)}, u32[]{:S(2)}) %collective-permute-start) | collective-permute-done | bytes 524320 | tf_op jit(solution)/shard_map/ppermute | solution.py:20
  24.3 1.1 constant_dynamic-update-slice_fusion.2
  25.4 1.5 constant_dynamic-update-slice_fusion.1
  26.9 10.0 %collective-permute-done.1 = bf16[128,1,16,128]{3,0,2,1:T(8,128)(2,1)S(1)} collective-permute-done((bf16[128,1,16,128]{3,0,2,1:T(8,128)(2,1)S(1)}, bf16[128,1,16,128]{3,0,2,1:T(8,128)(2,1)S(1)}, u32[]{:S(2)}, u32[]{:S(2)}) %collective-permute-start.1) | collective-permute-done | bytes 524320 | tf_op jit(solution)/shard_map/ppermute | solution.py:22
  37.0 6.3 collective-permute-start.2
  43.3 1.9 collective-permute-start.3
  45.3 0.6 collective-permute-done.2
  46.0 7.4 collective-permute-done.3
  53.3 0.6 maximum_convert_fusion
  53.9 3.1 fusion.14
  57.0 2.2 fusion.19
  59.2 3.8 pad_maximum_fusion
  63.0 12.0 %copy.17 = bf16[4,128,4,16,128]{4,3,2,1,0:T(8,128)(2,1)} copy(bf16[4,128,4,16,128]{4,1,3,2,0:T(8,128)(2,1)} %pad_maximum_fusion) | data formatting | bytes 16777216 | tf_op jit(solution)/shard_map/stack | solution.py:72
  75.1 13.3 %convert_element_type.36 = bf16[512,8192]{1,0:T(8,128)(2,1)} reshape(bf16[4,128,4,16,128]{4,3,2,1,0:T(8,128)(2,1)} %copy.17) | data formatting | bytes 16777216 | tf_op jit(solution)/shard_map/convert_element_type | solution.py:75
  88.4 50.1 %while.16 = (s32[]{:T(128)}, f32[1024,512]{1,0:T(8,128)}, f32[1024]{0:T(1024)S(1)}, s32[4,8192]{1,0:T(4,128)S(1)}, bf16[4,8192]{1,0:T(4,128)(2,1)S(1)}, /*index=...) while((s32[]{:T(128)}, f32[1024,512]{1,0:T(8,128)}, ...), condition=%wide.region_1.2_spmd.clone, body=%wide.region_0.1_spmd.clone.sunk | while | flops 1078986752 | bytes 11651254 | solution.py:100
  88.4 0.4 fusion.60
  88.8 3.8 select_add_fusion.4
  92.7 0.7 dynamic_slice.43
  93.4 0.6 fusion.61
  94.1 0.4 fusion.60
  94.5 4.5 select_add_fusion.4
  99.0 0.7 dynamic_slice.43
  99.7 0.6 fusion.61
  100.4 0.4 fusion.60
  100.8 4.5 select_add_fusion.4
  105.4 0.7 dynamic_slice.43
  106.1 0.6 fusion.61
  106.8 0.4 fusion.60
  107.2 4.5 select_add_fusion.4
  111.7 0.7 dynamic_slice.43
  112.4 0.6 fusion.61
  113.1 0.4 fusion.60
  113.5 4.5 select_add_fusion.4
  118.1 0.7 dynamic_slice.43
  118.8 0.6 fusion.61
  119.5 0.4 fusion.60
  119.9 4.5 select_add_fusion.4
  124.4 0.7 dynamic_slice.43
  125.1 0.6 fusion.61
  125.8 0.4 fusion.60
  126.2 4.5 select_add_fusion.4
  130.8 0.7 dynamic_slice.43
  131.5 0.6 fusion.61
  132.2 0.4 fusion.60
  132.6 4.5 select_add_fusion.4
  137.1 0.7 dynamic_slice.43
  137.8 0.6 fusion.61
  138.6 78.1 %psum.15 = f32[1024]{0:T(1024)S(1)} all-reduce(f32[1024]{0:T(1024)S(1)} %get-tuple-element.146), channel_id=1, replica_groups=mesh['narrow'=8,'wide'=32] {'narrow','wide'}, use_global_device_ids=true, to_apply=%region_5.6 | all-reduce | flops 1024 | bytes 8192 | tf_op jit(solution)/shard_map/psum | solution.py:101
  216.7 186.0 %all-reduce.3.cloned.1.call-done = f32[1024,512]{1,0:T(8,128)} async-done(((f32[1024,512]{1,0:T(8,128)}), f32[1024,512]{1,0:T(8,128)}) %all-reduce.3.cloned.1.call-update) | async-done | bytes 2097168 | tf_op jit(solution)/shard_map/psum | solution.py:101
  402.7 5.7 fusion.36
  408.4 1.3 reshape.187
  409.7 2.7 convolution_bitcast_fusion
  412.7 11.7 %custom-call.9 = f32[1,128,128]{2,1,0:T(8,128)S(1)} custom-call(f32[1,128,128]{2,1,0:T(8,128)S(1)} %fusion.29), custom_call_target="Cholesky" | custom-call | tf_op jit(solution)/shard_map/jit(cholesky)/cholesky | solution.py:54
  424.4 0.6 compare_reduce_fusion
  425.1 0.7 fusion.24
  425.7 9.8 %custom-call.10 = f32[1,1,128,128]{2,3,1,0:T(8,128)S(1)} custom-call(f32[1,1,128,128]{3,2,1,0:T(8,128)S(1)} %fusion.24), custom_call_target="InvertDiagBlocksLowerTriangular" | custom-call | tf_op jit(solution)/shard_map/triangular_solve | solution.py:58
  435.5 1.5 fusion.37
  437.5 344.6 %all-gather.1 = bf16[256,1,128]{2,1,0:T(2,128)(2,1)S(1)} all-gather(bf16[1,1,128]{2,1,0:T(2,128)(2,1)S(1)} %fusion.21), channel_id=2, replica_groups=mesh['narrow'=8,'wide'=32] {'narrow','wide'}, dimensions={0}, use_global_device_ids=true | all-gather | bytes 65792 | tf_op jit(solution)/shard_map/all_gather | solution.py:104
  782.1 5.6 fusion.13
  787.7 5.4 copy.27
  (81 shorter events, 1.6 us)
Async XLA Ops:
  6.5 18.8 %copy-start.1 = (bf16[128,4,16,128]{3,2,1,0:T(8,128)(2,1)S(1)}, bf16[128,4,16,128]{3,2,1,0:T(8,128)(2,1)}, u32[]{:S(2)}) copy-start(bf16[128,4,16,128]{3,2,1,0:T(8,128)(2,1)} %param.9) | copy-start | bytes 6291460
  6.5 9.1 %copy-start.2 = (s32[4,4,16,128]{3,2,1,0:T(8,128)S(1)}, s32[4,4,16,128]{3,2,1,0:T(8,128)}, u32[]{:S(2)}) copy-start(s32[4,4,16,128]{3,2,1,0:T(8,128)} %param.13) | copy-start | bytes 393220
  6.5 9.2 %copy-start.3 = (s32[4,4,16,128]{3,2,1,0:T(8,128)S(1)}, s32[4,4,16,128]{3,2,1,0:T(8,128)}, u32[]{:S(2)}) copy-start(s32[4,4,16,128]{3,2,1,0:T(8,128)} %param.12) | copy-start | bytes 393220
  6.5 396.1 %all-reduce.3.cloned.1.call-start = ((), (), s32[]{:S(2)}) async-start(), calls=%async_computation | async-start | bytes 4194304 | tf_op jit(solution)/shard_map/psum | solution.py:101
  9.0 15.3 %collective-permute-start = (bf16[128,1,16,128]{3,0,2,1:T(8,128)(2,1)}, bf16[128,1,16,128]{3,0,2,1:T(8,128)(2,1)}, u32[]{:S(2)}, u32[]{:S(2)}) collective-permute-start(bf16[128,1,16,128]{3,0,2,1:T(8,128)(2,1)} %copy.40), channel_id=1, source_target_pairs={{0,32},{32,64},{64,96},{96,128},{128,160},{160,192},{192,224},{1,3... | collective-permute-start | bytes 1572872 | tf_op jit(solution)/shard_map/ppermute | solution.py:20
  14.3 22.6 %collective-permute-start.1 = (bf16[128,1,16,128]{3,0,2,1:T(8,128)(2,1)S(1)}, bf16[128,1,16,128]{3,0,2,1:T(8,128)(2,1)S(1)}, u32[]{:S(2)}, u32[]{:S(2)}) collective-permute-start(bf16[128,1,16,128]{3,0,2,1:T(8,128)(2,1)S(1)} %copy.41), channel_id=1, source_target_pairs={{32,0},{64,32},{96,64},{128,96},{160,128},{192,160},{224,192},{33,... | collective-permute-start | bytes 1572872 | tf_op jit(solution)/shard_map/ppermute | solution.py:22
  25.4 19.9 %copy-start.4 = (f32[4,4,16,128]{3,2,1,0:T(8,128)S(1)}, f32[4,4,16,128]{3,2,1,0:T(8,128)}, u32[]{:S(2)}) copy-start(f32[4,4,16,128]{3,2,1,0:T(8,128)} %param.11) | copy-start | bytes 393220
  37.0 8.9 %collective-permute-start.2 = (bf16[128,6,1,128]{3,0,2,1:T(8,128)(2,1)S(1)}, bf16[128,6,1,128]{3,0,2,1:T(8,128)(2,1)S(1)}, u32[]{:S(2)}, u32[]{:S(2)}) collective-permute-start(bf16[128,6,1,128]{3,0,2,1:T(8,128)(2,1)S(1)} %get-tuple-element.191), channel_id=1, source_target_pairs={{0,1},{1,2},{2,3},{3,4},{4,5},{5,6},{6,7},{7,8},{8,9},{9,10},{10,1... | collective-permute-start | bytes 589832 | tf_op jit(solution)/shard_map/ppermute | solution.py:20
  43.3 10.0 %collective-permute-start.3 = (bf16[128,6,1,128]{3,0,2,1:T(8,128)(2,1)S(1)}, bf16[128,6,1,128]{3,0,2,1:T(8,128)(2,1)S(1)}, u32[]{:S(2)}, u32[]{:S(2)}) collective-permute-start(bf16[128,6,1,128]{3,0,2,1:T(8,128)(2,1)S(1)} %get-tuple-element.192), channel_id=1, source_target_pairs={{1,0},{2,1},{3,2},{4,3},{5,4},{6,5},{7,6},{8,7},{9,8},{10,9},{11,1... | collective-permute-start | bytes 589832 | tf_op jit(solution)/shard_map/ppermute | solution.py:22
  88.4 50.1 %copy-start.5 = (f32[1,4]{1,0:T(1,128)S(1)}, f32[1,4]{1,0:T(1,128)}, u32[]{:S(2)}) copy-start(f32[1,4]{1,0:T(1,128)} %param.14) | copy-start | bytes 52
  408.4 27.2 %copy-start = (f32[1024,512]{1,0:T(8,128)S(1)}, f32[1024,512]{1,0:T(8,128)}, u32[]{:S(2)}) copy-start(f32[1024,512]{1,0:T(8,128)} %all-reduce.3.cloned.1.call-done) | copy-start | bytes 6291460
  408.4 373.7 %copy-start.6 = (s32[256]{0:T(256)S(1)}, s32[256]{0:T(256)}, u32[]{:S(2)}) copy-start(s32[256]{0:T(256)} %param.15) | copy-start | bytes 3076
Sparse Core Ops, SparseCore 0:
  138.6 263.9 all-reduce.2
where the time goes:
time: 801 us; the launch traced here: 800 us
  blocking collectives  423 us (53%)
  waiting for transfers between devices  213 us (27%)
  matrix products  56.7 us (7%)
  local copies, waits for them, and re-layouts  43.4 us (5%)
  other arithmetic  36 us (4%)
  starting transfers between devices  14.7 us (2%)
  between operations  13.6 us (2%)
    all_gather x1, blocking collectives, per_device(): all_coef = lax.all_gather(own_coef, ('narrow', 'wide'), axis=0, tiled=True)  345 us
    psum x1, waiting for transfers between devices, per_device(): lax.psum((sketched, sketched_rhs), ('narrow', 'wide'))  186 us
    psum x1, blocking collectives, per_device(): lax.psum((sketched, sketched_rhs), ('narrow', 'wide'))  78.1 us
    dot_general x8, matrix products, accumulate(): lax.dot_general(hashed, columns, (((1,), (1,)), ((), ())), preferred_elem...  35.6 us
    ppermute x2, waiting for transfers between devices, extended(): lax.ppermute(head, axis, [((i + 1) % count, i) for i in range(ends)])  17.4 us
  transfers between devices with their start and end apart: 5, of which 5 were waited for; matrix products, arithmetic and copies ran while one was open for 0% of the time, Pallas kernels for 0%

commit v1 on v0

--- a/solution.py
+++ b/solution.py
@@ -98,7 +98,7 @@
 
     start = (jnp.zeros((M, TERMS * K), jnp.float32), jnp.zeros((M,), jnp.float32))
     sketched, sketched_rhs = lax.fori_loop(0, block_count, accumulate, start)
-    sketched, sketched_rhs = lax.psum((sketched, sketched_rhs), ("narrow", "wide"))
+    sketched, sketched_rhs = lax.psum(lax.psum((sketched, sketched_rhs), "narrow"), "wide")
     gram_matrix, projected = column_products(sketched, sketched_rhs)
     own_coef = solve_points(params, gram_matrix, projected).astype(jnp.bfloat16)
     all_coef = lax.all_gather(own_coef, ("narrow", "wide"), axis=0, tiled=True)

time: 801 us -> 938 us (1.17)
  waiting for transfers between devices: 213 us -> 342 us
    psum x1 -> x2, waiting for transfers between devices: 186 us -> 315 us  [the longest x1 205 us: per_device(): lax.psum(lax.psum((sketched, sketched_rhs), 'narrow'), 'wide')]
    psum x1 -> x2, blocking collectives: 78.1 us -> 88.3 us  [the longest x1 74.6 us: per_device(): lax.psum(lax.psum((sketched, sketched_rhs), 'narrow'), 'wide')]
  transfers between devices with their start and end apart: 5 -> 6, of which waited for: 5 -> 6; matrix products, arithmetic and copies ran while one was open for 0% -> 0% of each run, Pallas kernels for 0% -> 0%
where the time goes in v1:
time: 938 us; the launch traced here: 937 us
  blocking collectives  430 us (46%)
  waiting for transfers between devices  342 us (36%)
  matrix products  56.7 us (6%)
  local copies, waits for them, and re-layouts  43.4 us (5%)
  other arithmetic  36 us (4%)
  starting transfers between devices  14.7 us (2%)
  between operations  13.7 us (1%)
    all_gather x1, blocking collectives, per_device(): all_coef = lax.all_gather(own_coef, ('narrow', 'wide'), axis=0, tiled=True)  342 us
    psum x1, waiting for transfers between devices, per_device(): lax.psum(lax.psum((sketched, sketched_rhs), 'narrow'), 'wide')  205 us
    psum x1, waiting for transfers between devices, per_device(): lax.psum((sketched, sketched_rhs), 'narrow')  110 us
    psum x1, blocking collectives, per_device(): lax.psum(lax.psum((sketched, sketched_rhs), 'narrow'), 'wide')  74.6 us
    dot_general x8, matrix products, accumulate(): lax.dot_general(hashed, columns, (((1,), (1,)), ((), ())), preferred_elem...  35.6 us
  transfers between devices with their start and end apart: 6, of which 6 were waited for; matrix products, arithmetic and copies ran while one was open for 0% of the time, Pallas kernels for 0%

profile of v1, /device:TPU:1, one launch (start us, length us, event | category | flops | bytes accessed | tf_op | source)
XLA Modules:
  0.0 936.6 jit_solution(11918112970290243155)
XLA Ops:
  6.5 1.6 fusion.34
  8.1 0.9 copy.40
  9.0 5.2 collective-permute-start
  14.3 1.3 collective-permute-start.1
  15.9 8.4 collective-permute-done
  24.3 1.1 constant_dynamic-update-slice_fusion.2
  25.4 1.5 constant_dynamic-update-slice_fusion.1
  26.9 10.0 %collective-permute-done.1 = bf16[128,1,16,128]{3,0,2,1:T(8,128)(2,1)S(1)} collective-permute-done((bf16[128,1,16,128]{3,0,2,1:T(8,128)(2,1)S(1)}, bf16[128,1,16,128]{3,0,2,1:T(8,128)(2,1)S(1)}, u32[]{:S(2)}, u32[]{:S(2)}) %collective-permute-start.1) | collective-permute-done | bytes 524320 | tf_op jit(solution)/shard_map/ppermute | solution.py:22
  37.0 6.3 collective-permute-start.2
  43.4 1.9 collective-permute-start.3
  45.3 0.6 collective-permute-done.2
  46.0 7.4 collective-permute-done.3
  53.4 0.6 maximum_convert_fusion
  53.9 3.1 fusion.14
  57.0 2.2 fusion.19
  59.2 3.8 pad_maximum_fusion
  63.0 12.0 %copy.17 = bf16[4,128,4,16,128]{4,3,2,1,0:T(8,128)(2,1)} copy(bf16[4,128,4,16,128]{4,1,3,2,0:T(8,128)(2,1)} %pad_maximum_fusion) | data formatting | bytes 16777216 | tf_op jit(solution)/shard_map/stack | solution.py:72
  75.1 13.3 %convert_element_type.36 = bf16[512,8192]{1,0:T(8,128)(2,1)} reshape(bf16[4,128,4,16,128]{4,3,2,1,0:T(8,128)(2,1)} %copy.17) | data formatting | bytes 16777216 | tf_op jit(solution)/shard_map/convert_element_type | solution.py:75
  88.4 50.1 %while.16 = (s32[]{:T(128)}, f32[1024,512]{1,0:T(8,128)}, f32[1024]{0:T(1024)S(1)}, s32[4,8192]{1,0:T(4,128)S(1)}, bf16[4,8192]{1,0:T(4,128)(2,1)S(1)}, /*index=...) while((s32[]{:T(128)}, f32[1024,512]{1,0:T(8,128)}, ...), condition=%wide.region_1.2_spmd.clone, body=%wide.region_0.1_spmd.clone.sunk | while | flops 1078986752 | bytes 11651254 | solution.py:100
  88.4 0.4 fusion.60
  88.8 3.8 select_add_fusion.4
  92.7 0.7 dynamic_slice.43
  93.4 0.6 fusion.61
  94.1 0.4 fusion.60
  94.5 4.5 select_add_fusion.4
  99.0 0.7 dynamic_slice.43
  99.7 0.6 fusion.61
  100.8 4.5 select_add_fusion.4
  105.4 0.7 dynamic_slice.43
  106.1 0.6 fusion.61
  106.8 0.4 fusion.60
  107.2 4.5 select_add_fusion.4
  111.7 0.7 dynamic_slice.43
  112.4 0.6 fusion.61
  113.1 0.4 fusion.60
  113.5 4.5 select_add_fusion.4
  118.1 0.7 dynamic_slice.43
  118.8 0.6 fusion.61
  119.9 4.5 select_add_fusion.4
  124.4 0.7 dynamic_slice.43
  125.1 0.6 fusion.61
  125.8 0.4 fusion.60
  126.2 4.5 select_add_fusion.4
  130.8 0.7 dynamic_slice.43
  131.5 0.6 fusion.61
  132.2 0.4 fusion.60
  132.6 4.5 select_add_fusion.4
  137.1 0.7 dynamic_slice.43
  137.8 0.6 fusion.61
  138.5 110.2 %all-reduce.4.cloned.1.call-done = f32[1024,512]{1,0:T(8,128)} async-done(((f32[1024,512]{1,0:T(8,128)}), f32[1024,512]{1,0:T(8,128)}) %all-reduce.4.cloned.1.call-update) | async-done | bytes 2097168 | tf_op jit(solution)/shard_map/psum | solution.py:101
  248.9 13.7 %psum.30 = f32[1024]{0:T(1024)S(1)} all-reduce(f32[1024]{0:T(1024)S(1)} %get-tuple-element.146), channel_id=1, replica_groups=mesh['narrow'=8,'wide'=32] {'narrow'}, use_global_device_ids=true, to_apply=%region_6.7 | all-reduce | flops 1024 | bytes 8192 | tf_op jit(solution)/shard_map/psum | solution.py:101
  262.6 74.6 %psum.31 = f32[1024]{0:T(1024)S(1)} all-reduce(f32[1024]{0:T(1024)S(1)} %psum.30), channel_id=1, replica_groups=mesh['narrow'=8,'wide'=32] {'wide'}, use_global_device_ids=true, to_apply=%region_7.8 | all-reduce | flops 1024 | bytes 8192 | tf_op jit(solution)/shard_map/psum | solution.py:101
  337.2 205.2 %all-reduce.6.cloned.1.call-done = f32[1024,512]{1,0:T(8,128)} async-done(((f32[1024,512]{1,0:T(8,128)}), f32[1024,512]{1,0:T(8,128)}) %all-reduce.6.cloned.1.call-update) | async-done | bytes 2097168 | tf_op jit(solution)/shard_map/psum | solution.py:101
  542.4 5.7 fusion.36
  548.2 1.3 reshape.187
  549.5 2.7 convolution_bitcast_fusion
  552.4 11.7 %custom-call.9 = f32[1,128,128]{2,1,0:T(8,128)S(1)} custom-call(f32[1,128,128]{2,1,0:T(8,128)S(1)} %fusion.29), custom_call_target="Cholesky" | custom-call | tf_op jit(solution)/shard_map/jit(cholesky)/cholesky | solution.py:54
  564.2 0.6 compare_reduce_fusion
  564.8 0.7 fusion.24
  565.5 9.8 %custom-call.10 = f32[1,1,128,128]{2,3,1,0:T(8,128)S(1)} custom-call(f32[1,1,128,128]{3,2,1,0:T(8,128)S(1)} %fusion.24), custom_call_target="InvertDiagBlocksLowerTriangular" | custom-call | tf_op jit(solution)/shard_map/triangular_solve | solution.py:58
  575.3 1.5 fusion.37
  577.3 341.5 %all-gather.1 = bf16[256,1,128]{2,1,0:T(2,128)(2,1)S(1)} all-gather(bf16[1,1,128]{2,1,0:T(2,128)(2,1)S(1)} %fusion.21), channel_id=2, replica_groups=mesh['narrow'=8,'wide'=32] {'narrow','wide'}, dimensions={0}, use_global_device_ids=true | all-gather | bytes 65792 | tf_op jit(solution)/shard_map/all_gather | solution.py:104
  918.8 5.6 fusion.13
  924.4 5.4 copy.27
  (85 shorter events, 2.5 us)
Async XLA Ops:
  6.5 18.9 %copy-start.1 = (bf16[128,4,16,128]{3,2,1,0:T(8,128)(2,1)S(1)}, bf16[128,4,16,128]{3,2,1,0:T(8,128)(2,1)}, u32[]{:S(2)}) copy-start(bf16[128,4,16,128]{3,2,1,0:T(8,128)(2,1)} %param.9) | copy-start | bytes 6291460
  6.5 9.1 copy-start.2
  6.5 9.2 copy-start.3
  6.5 242.2 %all-reduce.4.cloned.1.call-start = ((), (), s32[]{:S(2)}) async-start(), calls=%async_computation | async-start | bytes 4194304 | tf_op jit(solution)/shard_map/psum | solution.py:101
  9.0 15.3 %collective-permute-start = (bf16[128,1,16,128]{3,0,2,1:T(8,128)(2,1)}, bf16[128,1,16,128]{3,0,2,1:T(8,128)(2,1)}, u32[]{:S(2)}, u32[]{:S(2)}) collective-permute-start(bf16[128,1,16,128]{3,0,2,1:T(8,128)(2,1)} %copy.40), channel_id=1, source_target_pairs={{0,32},{32,64},{64,96},{96,128},{128,160},{160,192},{192,224},{1,3... | collective-permute-start | bytes 1572872 | tf_op jit(solution)/shard_map/ppermute | solution.py:20
  14.3 22.6 %collective-permute-start.1 = (bf16[128,1,16,128]{3,0,2,1:T(8,128)(2,1)S(1)}, bf16[128,1,16,128]{3,0,2,1:T(8,128)(2,1)S(1)}, u32[]{:S(2)}, u32[]{:S(2)}) collective-permute-start(bf16[128,1,16,128]{3,0,2,1:T(8,128)(2,1)S(1)} %copy.41), channel_id=1, source_target_pairs={{32,0},{64,32},{96,64},{128,96},{160,128},{192,160},{224,192},{33,... | collective-permute-start | bytes 1572872 | tf_op jit(solution)/shard_map/ppermute | solution.py:22
  25.4 19.9 %copy-start.4 = (f32[4,4,16,128]{3,2,1,0:T(8,128)S(1)}, f32[4,4,16,128]{3,2,1,0:T(8,128)}, u32[]{:S(2)}) copy-start(f32[4,4,16,128]{3,2,1,0:T(8,128)} %param.11) | copy-start | bytes 393220
  37.0 8.9 collective-permute-start.2
  43.4 10.0 %collective-permute-start.3 = (bf16[128,6,1,128]{3,0,2,1:T(8,128)(2,1)S(1)}, bf16[128,6,1,128]{3,0,2,1:T(8,128)(2,1)S(1)}, u32[]{:S(2)}, u32[]{:S(2)}) collective-permute-start(bf16[128,6,1,128]{3,0,2,1:T(8,128)(2,1)S(1)} %get-tuple-element.192), channel_id=1, source_target_pairs={{1,0},{2,1},{3,2},{4,3},{5,4},{6,5},{7,6},{8,7},{9,8},{10,9},{11,1... | collective-permute-start | bytes 589832 | tf_op jit(solution)/shard_map/ppermute | solution.py:22
  138.5 110.4 %copy-start.5 = (f32[1,4]{1,0:T(1,128)S(1)}, f32[1,4]{1,0:T(1,128)}, u32[]{:S(2)}) copy-start(f32[1,4]{1,0:T(1,128)} %param.14) | copy-start | bytes 52
  138.5 403.9 %all-reduce.6.cloned.1.call-start = ((), (), s32[]{:S(2)}) async-start(), calls=%async_computation.1 | async-start | bytes 4194304 | tf_op jit(solution)/shard_map/psum | solution.py:101
  548.2 27.2 %copy-start = (f32[1024,512]{1,0:T(8,128)S(1)}, f32[1024,512]{1,0:T(8,128)}, u32[]{:S(2)}) copy-start(f32[1024,512]{1,0:T(8,128)} %all-reduce.6.cloned.1.call-done) | copy-start | bytes 6291460
  548.2 370.6 %copy-start.6 = (s32[256]{0:T(256)S(1)}, s32[256]{0:T(256)}, u32[]{:S(2)}) copy-start(s32[256]{0:T(256)} %param.15) | copy-start | bytes 3076
Sparse Core Ops, SparseCore 0:
  138.6 110.1 all-reduce.3
  251.4 290.9 all-reduce.5
